TPU v7x, 32 devices: a whole 2x2x4 slice. The times are simulated.
32 devices in a mesh: dp: 4 (over x, core), ctx: 4 (over z), tensor: 2 (over y).
Axes of the slice: x: 2, y: 2, z: 4, core: 2. Of those that a mesh axis runs over, the one named last changes fastest.
Arguments:
- block_input: bfloat16 [12288, 2048], P(('dp', 'ctx'), 'tensor'), may hold values from -6 to 6
- cotangent: bfloat16 [12288, 2048], P(('dp', 'ctx'), 'tensor'), may hold values from -6 to 6
- deal_order: int32 [4, 4], P('dp'), may hold values from 0 to 3, as said below
- seq_lengths: int32 [12], P('dp'), may hold values from 96 to 2880, as said below
- seq_adapter: int32 [12], P('dp'), may hold values from 0 to 7
- mixer_gain: bfloat16 [2048], replicated, may hold values from 0.099609375 to 1.8984375
- ffn_gain: bfloat16 [2048], replicated, may hold values from 0.099609375 to 1.8984375
- conv_taps: bfloat16 [3, 2048], P(None, 'tensor'), may hold values from -3.5 to 3.5
- in_weight: bfloat16 [3, 2048, 2048], P(None, 'dp', 'tensor'), may hold values from -0.125 to 0.125
- out_weight: bfloat16 [2048, 2048], P('tensor', 'dp'), may hold values from -0.125 to 0.125
- gateup_weight: bfloat16 [2, 2048, 5632], P(None, 'dp', 'tensor'), may hold values from -0.125 to 0.125
- down_weight: bfloat16 [5632, 2048], P('tensor', 'dp'), may hold values from -0.078125 to 0.078125
- input_adapter_shrink: bfloat16 [2048, 128], replicated, may hold values from -0.125 to 0.125
- in_expand: bfloat16 [3, 128, 2048], P(None, None, 'tensor'), may hold values from -1.5 to 1.5
- out_shrink: bfloat16 [2048, 128], P('tensor'), may hold values from -0.125 to 0.125
- output_adapter_expand: bfloat16 [128, 2048], replicated, may hold values from -1.5 to 1.5
- ffn_shrink: bfloat16 [2048, 256], replicated, may hold values from -0.125 to 0.125
- ffn_expand: bfloat16 [2, 128, 5632], P(None, None, 'tensor'), may hold values from -1.5 to 1.5
- down_shrink: bfloat16 [5632, 128], P('tensor'), may hold values from -0.078125 to 0.078125
- down_adapter_expand: bfloat16 [128, 2048], replicated, may hold values from -1.5 to 1.5
Outputs:
- block_output: bfloat16 [12288, 2048], P(('dp', 'ctx'), 'tensor')
- input_grad: float32 [12288, 2048], P(('dp', 'ctx'), 'tensor')
- in_shrink_grad: float32 [2048, 128], replicated
- input_expand_gradient: float32 [3, 128, 2048], P(None, None, 'tensor')
- out_shrink_grad: float32 [2048, 128], P('tensor')
- output_expand_gradient: float32 [128, 2048], replicated
- ffn_shrink_grad: float32 [2048, 256], replicated
- feedforward_expand_gradient: float32 [2, 128, 5632], P(None, None, 'tensor')
- down_shrink_grad: float32 [5632, 128], P('tensor')
- down_adapter_expand_gradient: float32 [128, 2048], replicated
Inputs may be any that keep to these rules, and one draw needn't show every extreme that they name: `deal_order`: each row is a permutation of the 4 shard numbers. `seq_lengths`: each data group's 3 entries sum to 3072; all but one of them lie between 96 and 192.
All inputs are finite; a program needn't handle non-finite values.
Results may differ from a plain program's by a relative error of at most 0.013.
Values may be sent and summed in bfloat16 or wider, within the bound.
No kernel may reach another device: no remote copies, remote signals or barrier semaphores. Data moves between devices by JAX's collectives and lax.ppermute only.
A program may use at most 256 MiB of HBM per device.

v0:
```python
import jax
import jax.numpy as jnp
from jax import lax
from jax.sharding import PartitionSpec as P

RANK = 16
norm_eps = 1e-05
adapter_scale = 0.5


def shifted(block, axis, distance):
    devices = range(lax.axis_size(axis))
    route = [(i - distance, i) for i in devices if i - distance in devices]
    return lax.ppermute(block, axis, route)


def rms_scale(values):
    return lax.rsqrt(jnp.mean(values * values, axis=-1, keepdims=True) + norm_eps)


def norm_back(values, scale, gain, grad_out):
    unit = values * scale
    grad_unit = grad_out * gain
    return scale * (grad_unit - unit * jnp.mean(grad_unit * unit, axis=-1, keepdims=True))


def product_simple(left, right):
    return jnp.dot(left, right, preferred_element_type=jnp.float32)


def product_backward(left, right):
    return lax.dot_general(
        left, right, (((1,), (1,)), ((), ())), preferred_element_type=jnp.float32
    )


def product_leading(left, right):
    return lax.dot_general(
        left, right, (((0,), (0,)), ((), ())), preferred_element_type=jnp.float32
    )


def segment_of(positions, seq_ends):
    return jnp.sum((positions[:, None] >= seq_ends[None, :]).astype(jnp.int32), axis=1)


def fetch_mixer(in_weight, out_weight):
    return (
        lax.all_gather(in_weight, "dp", axis=1, tiled=True),
        lax.all_gather(out_weight, "dp", axis=1, tiled=True),
    )


def fetch_ffn(gateup_weight, down_weight):
    return (
        lax.all_gather(gateup_weight, "dp", axis=1, tiled=True),
        lax.all_gather(down_weight, "dp", axis=1, tiled=True),
    )


def body(
    block_input,
    cotangent,
    deal_order,
    seq_lengths,
    seq_adapter,
    mixer_gain,
    ffn_gain,
    conv_taps,
    in_weight,
    out_weight,
    gateup_weight,
    down_weight,
    input_adapter_shrink,
    in_expand,
    out_shrink,
    output_adapter_expand,
    ffn_shrink,
    ffn_expand,
    down_shrink,
    down_adapter_expand,
):
    tok_count = block_input.shape[0]
    half_width = block_input.shape[1]
    rank_cols = input_adapter_shrink.shape[1]
    part_index = lax.axis_index("tensor")
    group_total = lax.axis_size("dp")
    block_rows = tok_count // group_total
    deal_row = deal_order[0]
    slot_all = jnp.arange(group_total, dtype=jnp.int32)
    inverse_row = jnp.sum(
        jnp.where(deal_row[:, None] == slot_all[None, :], slot_all[:, None], 0), axis=0
    )
    dealt_in, dealt_cot = (
        lax.all_to_all(
            block_input.reshape(group_total, block_rows, half_width),
            "dp",
            split_axis=0,
            concat_axis=0,
            tiled=True,
        ),
        lax.all_to_all(
            cotangent.reshape(group_total, block_rows, half_width),
            "dp",
            split_axis=0,
            concat_axis=0,
            tiled=True,
        ),
    )
    packed_in = jnp.take(dealt_in, deal_row, axis=0).reshape(tok_count, half_width)
    packed_cot = jnp.take(dealt_cot, deal_row, axis=0).reshape(tok_count, half_width)
    seq_ends = jnp.cumsum(seq_lengths)[:-1]
    positions = lax.axis_index("ctx") * tok_count + jnp.arange(tok_count, dtype=jnp.int32)
    segment = segment_of(positions, seq_ends)
    slot_ids = jnp.arange(seq_lengths.shape[0], dtype=jnp.int32)
    token_adapter_index = jnp.sum(
        jnp.where(segment[:, None] == slot_ids[None, :], seq_adapter[None, :], 0), axis=1
    )
    column_group_index = jnp.arange(rank_cols, dtype=jnp.int32) // RANK
    adapter_mask = (column_group_index[None, :] == token_adapter_index[:, None]).astype(jnp.float32)
    adapter_half_float = adapter_mask.astype(jnp.bfloat16)
    adapter_mask_pair = jnp.concatenate([adapter_mask, adapter_mask], axis=1)
    pair_bf = adapter_mask_pair.astype(jnp.bfloat16)
    matching_first = ((positions >= 1) & (segment_of(positions - 1, seq_ends) == segment)).astype(
        jnp.float32
    )[:, None]
    matching_second = ((positions >= 2) & (segment_of(positions - 2, seq_ends) == segment)).astype(
        jnp.float32
    )[:, None]
    ahead_one = (segment_of(positions + 1, seq_ends) == segment).astype(jnp.float32)[:, None]
    ahead_two = (segment_of(positions + 2, seq_ends) == segment).astype(jnp.float32)[:, None]
    row_pair = (
        lax.all_gather(packed_in, "tensor", axis=1, tiled=True),
        lax.all_gather(packed_cot, "tensor", axis=1, tiled=True),
    )
    input_complete = row_pair[0].astype(jnp.float32)
    cotangent_half_float = row_pair[1]
    cot_full = cotangent_half_float.astype(jnp.float32)
    mixer_f = mixer_gain.astype(jnp.float32)
    ffn_f = ffn_gain.astype(jnp.float32)
    conv_w = conv_taps.astype(jnp.float32)
    in_full, out_full = fetch_mixer(in_weight, out_weight)
    scale_one = rms_scale(input_complete)
    normalized_rows = (input_complete * scale_one * mixer_f).astype(jnp.bfloat16)
    input_rank_rows = (
        product_simple(normalized_rows, input_adapter_shrink).astype(jnp.bfloat16)
        * adapter_half_float
    )
    projected_rows = jnp.einsum(
        "px,sxa->psa", normalized_rows, in_full, preferred_element_type=jnp.float32
    ) + adapter_scale * jnp.einsum(
        "fw,kwo->fko", input_rank_rows, in_expand, preferred_element_type=jnp.float32
    )
    gate_b = projected_rows[:, 0]
    gate_c = projected_rows[:, 1]
    values_x = projected_rows[:, 2]
    mixed = (gate_b * values_x).astype(jnp.bfloat16)
    prior = shifted(mixed[tok_count - 2 :], "ctx", 1)
    extended = jnp.concatenate([prior, mixed], axis=0).astype(jnp.float32)
    conv_out = (
        conv_w[0] * extended[2:]
        + conv_w[1] * extended[1:-1] * matching_first
        + conv_w[2] * extended[:-2] * matching_second
    )
    gated_rows = (gate_c * conv_out).astype(jnp.bfloat16)
    adapter_branch_sum, output_rank_sum = lax.psum(
        (product_simple(gated_rows, out_full), product_simple(gated_rows, out_shrink)), "tensor"
    )
    output_rank_rows = output_rank_sum.astype(jnp.bfloat16) * adapter_half_float
    hidden_state_rows = input_complete + (
        adapter_branch_sum + adapter_scale * product_simple(output_rank_rows, output_adapter_expand)
    )
    scale_two = rms_scale(hidden_state_rows)
    feedforward_input = (hidden_state_rows * scale_two * ffn_f).astype(jnp.bfloat16)
    feedforward_rank_rows = (
        product_simple(feedforward_input, ffn_shrink).astype(jnp.bfloat16) * pair_bf
    )
    ffn_low_split = feedforward_rank_rows.reshape(tok_count, 2, rank_cols)
    gu_full, down_full = fetch_ffn(gateup_weight, down_weight)
    gate_up_output = jnp.einsum(
        "cm,ame->cae", feedforward_input, gu_full, preferred_element_type=jnp.float32
    ) + adapter_scale * jnp.einsum(
        "vmc,mcb->vmb", ffn_low_split, ffn_expand, preferred_element_type=jnp.float32
    )
    gate_pre = gate_up_output[:, 0]
    up_pre = gate_up_output[:, 1]
    activated_rows = (jax.nn.silu(gate_pre) * up_pre).astype(jnp.bfloat16)
    down_weight_slice = lax.psum_scatter(
        product_simple(activated_rows, down_full).astype(jnp.bfloat16),
        "tensor",
        scatter_dimension=1,
        tiled=True,
    ).astype(jnp.float32)
    down_rank_rows_sum = lax.psum(product_simple(activated_rows, down_shrink), "tensor")
    down_rank_rows = down_rank_rows_sum.astype(jnp.bfloat16) * adapter_half_float
    expand_factor_slice = lax.dynamic_slice_in_dim(
        down_adapter_expand, part_index * half_width, half_width, 1
    )
    hidden_column_slice = lax.dynamic_slice_in_dim(
        hidden_state_rows, part_index * half_width, half_width, 1
    )
    packed_output = (
        hidden_column_slice
        + (down_weight_slice + adapter_scale * product_simple(down_rank_rows, expand_factor_slice))
    ).astype(jnp.bfloat16)
    gu_full, down_full = fetch_ffn(gateup_weight, down_weight)
    down_rank_gradient = (
        adapter_scale * product_backward(cotangent_half_float, down_adapter_expand) * adapter_mask
    ).astype(jnp.bfloat16)
    down_adapter_expand_gradient = adapter_scale * product_leading(
        down_rank_rows, cotangent_half_float
    )
    grad_act = product_backward(cotangent_half_float, down_full) + product_backward(
        down_rank_gradient, down_shrink
    )
    down_shrink_grad = product_leading(activated_rows, down_rank_gradient)
    sigmoid_gate = jax.nn.sigmoid(gate_pre)
    grad_gate = grad_act * up_pre * sigmoid_gate * (1.0 + gate_pre * (1.0 - sigmoid_gate))
    grad_up = grad_act * gate_pre * sigmoid_gate
    grad_gu = jnp.stack([grad_gate, grad_up], axis=1).astype(jnp.bfloat16)
    feedforward_expand_gradient = adapter_scale * jnp.einsum(
        "tje,tjf->jef", ffn_low_split, grad_gu, preferred_element_type=jnp.float32
    )
    feedforward_rank_part = adapter_scale * jnp.einsum(
        "tjf,jef->tje", grad_gu, ffn_expand, preferred_element_type=jnp.float32
    ).reshape(tok_count, 2 * rank_cols)
    ffn_in_part = jnp.einsum("tjf,jdf->td", grad_gu, gu_full, preferred_element_type=jnp.float32)
    ffn_in_sum, ffn_low_sum = lax.psum((ffn_in_part, feedforward_rank_part), "tensor")
    grad_ffn_low = (ffn_low_sum * adapter_mask_pair).astype(jnp.bfloat16)
    grad_ffn_in = ffn_in_sum + product_backward(grad_ffn_low, ffn_shrink)
    ffn_shrink_grad = product_leading(feedforward_input, grad_ffn_low)
    grad_hidden = cot_full + norm_back(hidden_state_rows, scale_two, ffn_f, grad_ffn_in)
    in_full, out_full = fetch_mixer(in_weight, out_weight)
    adapter_branch_gradient = grad_hidden.astype(jnp.bfloat16)
    out_rank_gradient = (
        adapter_scale
        * product_backward(adapter_branch_gradient, output_adapter_expand)
        * adapter_mask
    ).astype(jnp.bfloat16)
    output_expand_gradient = adapter_scale * product_leading(
        output_rank_rows, adapter_branch_gradient
    )
    grad_gated = product_backward(adapter_branch_gradient, out_full) + product_backward(
        out_rank_gradient, out_shrink
    )
    out_shrink_grad = product_leading(gated_rows, out_rank_gradient)
    grad_gate_c = grad_gated * conv_out
    grad_conv = grad_gated * gate_c
    ahead = shifted(grad_conv[:2], "ctx", -1)
    trailing = jnp.concatenate([grad_conv, ahead], axis=0)
    grad_mixed = (
        conv_w[0] * grad_conv
        + conv_w[1] * trailing[1:-1] * ahead_one
        + conv_w[2] * trailing[2:] * ahead_two
    )
    grad_proj = jnp.stack([grad_mixed * values_x, grad_gate_c, grad_mixed * gate_b], axis=1).astype(
        jnp.bfloat16
    )
    input_expand_gradient = adapter_scale * jnp.einsum(
        "te,tjc->jec", input_rank_rows, grad_proj, preferred_element_type=jnp.float32
    )
    input_rank_part = adapter_scale * jnp.einsum(
        "tjc,jec->te", grad_proj, in_expand, preferred_element_type=jnp.float32
    )
    normed_part = jnp.einsum("tjc,jdc->td", grad_proj, in_full, preferred_element_type=jnp.float32)
    normed_sum, input_rank_sum = lax.psum((normed_part, input_rank_part), "tensor")
    in_rank_gradient = (input_rank_sum * adapter_mask).astype(jnp.bfloat16)
    grad_normed = normed_sum + product_backward(in_rank_gradient, input_adapter_shrink)
    in_shrink_grad = product_leading(normalized_rows, in_rank_gradient)
    grad_input_full = grad_hidden + norm_back(input_complete, scale_one, mixer_f, grad_normed)
    packed_grad = lax.dynamic_slice_in_dim(grad_input_full, part_index * half_width, half_width, 1)
    output_blocks = jnp.take(
        packed_output.reshape(group_total, block_rows, half_width), inverse_row, axis=0
    )
    grad_blocks = jnp.take(
        packed_grad.reshape(group_total, block_rows, half_width), inverse_row, axis=0
    )
    block_output = lax.all_to_all(
        output_blocks, "dp", split_axis=0, concat_axis=0, tiled=True
    ).reshape(tok_count, half_width)
    input_grad = (
        lax.all_to_all(
            grad_blocks.astype(jnp.bfloat16), "dp", split_axis=0, concat_axis=0, tiled=True
        )
        .astype(grad_blocks.dtype)
        .reshape(tok_count, half_width)
    )
    totals = lax.psum(
        (
            in_shrink_grad,
            input_expand_gradient,
            out_shrink_grad,
            output_expand_gradient,
            ffn_shrink_grad,
            feedforward_expand_gradient,
            down_shrink_grad,
            down_adapter_expand_gradient,
        ),
        ("dp", "ctx"),
    )
    return (
        block_output,
        input_grad,
        totals[0],
        totals[1],
        totals[2],
        totals[3],
        totals[4],
        totals[5],
        totals[6],
        totals[7],
    )


def solution(mesh):
    placed = (
        P(("dp", "ctx"), "tensor"),
        P(("dp", "ctx"), "tensor"),
        P("dp", None),
        P("dp"),
        P("dp"),
        P(),
        P(),
        P(None, "tensor"),
        P(None, "dp", "tensor"),
        P("tensor", "dp"),
        P(None, "dp", "tensor"),
        P("tensor", "dp"),
        P(),
        P(None, None, "tensor"),
        P("tensor", None),
        P(),
        P(),
        P(None, None, "tensor"),
        P("tensor", None),
        P(),
    )
    return jax.shard_map(
        body,
        mesh=mesh,
        in_specs=placed,
        out_specs=(
            P(("dp", "ctx"), "tensor"),
            P(("dp", "ctx"), "tensor"),
            P(),
            P(None, None, "tensor"),
            P("tensor", None),
            P(),
            P(),
            P(None, None, "tensor"),
            P("tensor", None),
            P(),
        ),
        check_vma=False,
    )
```

profile of v0, /device:TPU:0, one launch (start us, length us, event | category | flops | bytes accessed | tf_op | source)
XLA Modules:
  0.0 1380.1 jit_solution(14482190222094816660)
XLA Ops:
  7.2 25.2 %all_to_all.20 = bf16[4,192,1024]{2,1,0:T(8,128)(2,1)} all-to-all(bf16[4,192,1024]{2,1,0:T(8,128)(2,1)} %bitcast.155), channel_id=1, replica_groups=mesh['dp'=4,'ctx'=4,'tensor'=2] {'dp'}, dimensions={0} | all-to-all | bytes 3145728 | tf_op jit(solution)/shard_map/all_to_all | solution.py:95
  39.3 16.7 %all-to-all-done.2 = bf16[4,192,1024]{2,1,0:T(8,128)(2,1)S(1)} async-done(((bf16[4,192,1024]{2,1,0:T(8,128)(2,1)}), bf16[4,192,1024]{2,1,0:T(8,128)(2,1)S(1)}, u32[]{:S(2)}, u32[]{:S(2)}) %all-to-all-start.2) | async-done | bytes 1572896 | tf_op jit(solution)/shard_map/all_to_all | solution.py:102
  65.6 42.4 %all-gather.7.cloned.1.call-done = bf16[768,2048]{1,0:T(8,128)(2,1)} async-done(((bf16[768,1024]{1,0:T(8,128)(2,1)}), bf16[768,2048]{1,0:T(8,128)(2,1)}) %all-gather.7.cloned.1.call-update) | async-done | bytes 3145744 | tf_op jit(solution)/shard_map/all_gather | solution.py:133
  111.9 79.8 %all-gather.9.cloned.1.call-done = bf16[3,2048,1024]{2,1,0:T(8,128)(2,1)} async-done(((bf16[3,512,1024]{2,1,0:T(8,128)(2,1)}), bf16[3,2048,1024]{2,1,0:T(8,128)(2,1)}) %all-gather.9.cloned.1.call-update) | async-done | bytes 12582928 | tf_op jit(solution)/shard_map/all_gather | solution.py:49
  191.7 13.6 fusion.17
  215.4 12.4 all-gather.11.cloned.1.call-done
  227.8 7.4 fusion.72
  237.9 36.9 %all-gather.17.cloned.1.call-done = bf16[768,2048]{1,0:T(8,128)(2,1)} async-done(((bf16[768,1024]{1,0:T(8,128)(2,1)}), bf16[768,2048]{1,0:T(8,128)(2,1)}) %all-gather.17.cloned.1.call-update) | async-done | bytes 3145744 | tf_op jit(solution)/shard_map/all_gather | solution.py:134
  278.3 74.0 %all-gather.15.cloned.1.call-done = bf16[2816,2048]{1,0:T(8,128)(2,1)} async-done(((bf16[2816,512]{1,0:T(8,128)(2,1)}), bf16[2816,2048]{1,0:T(8,128)(2,1)}) %all-gather.15.cloned.1.call-update) | async-done | bytes 11534352 | tf_op jit(solution)/shard_map/all_gather | solution.py:57
  352.3 15.8 %fusion.75 = f32[768,2816]{1,0:T(8,128)} fusion(bf16[768,2048]{1,0:T(8,128)(2,1)} %all-gather.17.cloned.1.call-done, bf16[2816,2048]{1,0:T(8,128)(2,1)} %all-gather.15.cloned.1.call-done), kind=kOutput, calls=%fused_computation.166 | convolution fusion | flops 8858370048 | bytes 23330816 | tf_op jit(solution)/shard_map/dot_general | solution.py:32
  369.5 25.5 %all-reduce.17 = bf16[768,128]{1,0:T(8,128)(2,1)S(1)} all-reduce(f32[768,128]{1,0:T(8,128)} %fusion.73), channel_id=1, replica_groups=mesh['dp'=4,'ctx'=4,'tensor'=2] {'tensor'}, use_global_device_ids=true, to_apply=%region_7.9 | all-reduce | flops 98304 | bytes 589824 | tf_op jit(solution)/shard_map/psum | solution.py:166
  395.0 121.3 %all-reduce.10.cloned.1.call-done = f32[768,2048]{1,0:T(8,128)} async-done(((f32[768,2048]{1,0:T(8,128)}), f32[768,2048]{1,0:T(8,128)}) %all-reduce.10.cloned.1.call-update) | async-done | bytes 6291472 | tf_op jit(solution)/shard_map/psum | solution.py:166
  516.3 4.7 multiply_reduce_fusion.2
  528.2 131.7 %all-gather.13.cloned.1.call-done = bf16[2,2048,2816]{2,1,0:T(8,128)(2,1)} async-done(((bf16[2,512,2816]{2,1,0:T(8,128)(2,1)}), bf16[2,2048,2816]{2,1,0:T(8,128)(2,1)}) %all-gather.13.cloned.1.call-update) | async-done | bytes 23068688 | tf_op jit(solution)/shard_map/all_gather | solution.py:56
  659.9 23.8 %fusion.15 = f32[768,2,2816]{2,0,1:T(8,128)S(1)} fusion(bf16[2,2048,2816]{2,1,0:T(8,128)(2,1)} %all-gather.13.cloned.1.call-done, bf16[768,2048]{1,0:T(8,128)(2,1)} %copy-done.11), kind=kOutput, calls=%fused_computation.57 | convolution fusion | flops 17716740096 | bytes 43515904 | tf_op jit(solution)/shard_map/cm,ame->cae/dot_general | solution.py:180
  683.6 9.4 bitcast_add_fusion
  693.0 13.5 fusion.2
  706.6 5.8 fusion.24
  713.6 25.4 %convolution_bitcast_fusion.1 = f32[768,2048]{1,0:T(8,128)} fusion(bf16[2,2048,2816]{2,1,0:T(8,128)(2,1)} %all-gather.13.cloned.1.call-done, bf16[768,1,2816]{2,0,1:T(8,128)(2,1)} %get-tuple-element.53, bf16[768,1,2816]{2,0,1:T(8,128)(2,1)} %copy-done.65), kind=kOutput, calls=%fused_computation.31 | convolution fusion | flops 17721065472 | bytes 38010880 | tf_op jit(solution)/shard_map/tjf,jdf->td/dot_general | solution.py:227
  739.0 14.4 %convolution_convert_fusion = bf16[768,2048]{1,0:T(8,128)(2,1)} fusion(bf16[768,2816]{1,0:T(8,128)(2,1)} %get-tuple-element.54, bf16[2816,2048]{1,0:T(8,128)(2,1)} %all-gather.15.cloned.1.call-done), kind=kOutput, calls=%fused_computation.32 | convolution fusion | flops 8859942912 | bytes 19005440 | tf_op jit(solution)/shard_map/dot_general | solution.py:28
  753.6 156.1 %all-reduce.16.cloned.1.call-done = (f32[768,2048]{1,0:T(8,128)}, f32[768,256]{1,0:T(8,128)}) async-done(((f32[768,2048]{1,0:T(8,128)}, f32[768,256]{1,0:T(8,128)}), (f32[768,2048]{1,0:T(8,128)}, f32[768,256]{1,0:T(8,128)})) %all-reduce.16.cloned.1.call-update) | async-done | bytes 7077904 | tf_op jit(solution)/shard_map/psum | solution.py:228
  909.7 6.5 multiply_reduce_fusion.1
  930.6 4.2 collective-permute-done.1
  940.3 14.7 %convolution_bitcast_fusion = f32[768,2048]{1,0:T(8,128)} fusion(bf16[3,2048,1024]{2,1,0:T(8,128)(2,1)} %all-gather.9.cloned.1.call-done, bf16[768,1,1024]{2,0,1:T(8,128)(2,1)S(1)} %fusion.23, bf16[768,1,1024]{2,0,1:T(8,128)(2,1)S(1)} %get-tuple-element.57, bf16[768,1,1024]{2,0,1:T(8,128)(2,1)S(1)} %get-tuple-element.48), kind=kOutput, calls=%fused_computation.30 | convolution fusion | flops 9668395008 | bytes 23592960 | tf_op jit(solution)/shard_map/tjc,jdc->td/dot_general | solution.py:265
  959.1 4.8 fusion.77
  963.9 6.9 convolution_multiply_fusion
  978.8 41.3 %all-reduce.18 = (bf16[768,128]{1,0:T(8,128)(2,1)S(1)}, bf16[768,128]{1,0:T(8,128)(2,1)S(1)}) all-reduce(f32[768,128]{1,0:T(8,128)S(1)} %fusion.74, f32[768,128]{1,0:T(8,128)S(1)} %fusion.27), channel_id=1, replica_groups=mesh['dp'=4,'ctx'=4,'tensor'=2] {'tensor'}, use_global_device_ids=true, to_apply=%region_10.12 | all-reduce | flops 196608 | bytes 1179648 | tf_op jit(solution)/shard_map/psum | solution.py:194
  1035.0 92.8 %all-reduce.12.cloned.1.call-done = f32[768,2048]{1,0:T(8,128)} async-done(((f32[768,2048]{1,0:T(8,128)}), f32[768,2048]{1,0:T(8,128)}) %all-reduce.12.cloned.1.call-update) | async-done | bytes 6291472 | tf_op jit(solution)/shard_map/psum | solution.py:266
  1127.8 4.9 multiply_reduce_fusion
  1141.1 39.8 %all_to_all.21 = bf16[4,192,1024]{2,1,0:T(8,128)(2,1)S(1)} all-to-all(bf16[4,192,1024]{2,1,0:T(8,128)(2,1)S(1)} %get-tuple-element.67), channel_id=1, replica_groups=mesh['dp'=4,'ctx'=4,'tensor'=2] {'dp'}, dimensions={0} | all-to-all | bytes 3145728 | tf_op jit(solution)/shard_map/all_to_all | solution.py:278
  1180.9 4.4 all-to-all-start.3
  1185.3 170.9 %all-reduce.14.cloned.1.call-done = (f32[2048,128]{1,0:T(8,128)}, f32[3,128,1024]{1,2,0:T(8,128)}, f32[1024,128]{1,0:T(8,128)}, f32[128,2048]{1,0:T(8,128)}, f32...) async-done(((f32[2048,128]{1,0:T(8,128)}, f32[3,128,1024]{1,2,0:T(8,128)}, f32[1024,128]{1,0:T(8,128)}, ...) | async-done | bytes 11665424 | tf_op jit(solution)/shard_map/psum | solution.py:288
  (250 shorter events, 117.4 us)
Async XLA Ops:
  7.2 676.5 %copy-start = (bf16[2,128,2816]{2,1,0:T(8,128)(2,1)S(1)}, bf16[2,128,2816]{2,1,0:T(8,128)(2,1)}, u32[]{:S(2)}) copy-start(bf16[2,128,2816]{2,1,0:T(8,128)(2,1)} %param.39) | copy-start | bytes 4325380
  7.2 28.9 %copy-start.63 = (s32[1,4]{1,0:T(1,128)S(1)}, s32[1,4]{1,0:T(1,128)}, u32[]{:S(2)}) copy-start(s32[1,4]{1,0:T(1,128)} %param.24) | copy-start | bytes 52
  32.4 23.6 %all-to-all-start.2 = ((bf16[4,192,1024]{2,1,0:T(8,128)(2,1)}), bf16[4,192,1024]{2,1,0:T(8,128)(2,1)S(1)}, u32[]{:S(2)}, u32[]{:S(2)}) async-start(bf16[4,192,1024]{2,1,0:T(8,128)(2,1)} %bitcast.156), calls=%async_computation.3 | async-start | bytes 3145728 | tf_op jit(solution)/shard_map/all_to_all | solution.py:102
  36.0 72.0 %all-gather.7.cloned.1.call-start = ((), (), s32[]{:S(2)}) async-start(), calls=%async_computation.5 | async-start | bytes 4718592 | tf_op jit(solution)/shard_map/all_gather | solution.py:133
  61.8 130.0 %all-gather.9.cloned.1.call-start = ((), (), s32[]{:S(2)}) async-start(), calls=%async_computation.6 | async-start | bytes 15728640 | tf_op jit(solution)/shard_map/all_gather | solution.py:49
  62.6 165.3 %all-gather.11.cloned.1.call-start = ((), (), s32[]{:S(2)}) async-start(), calls=%async_computation.7 | async-start | bytes 5242880 | tf_op jit(solution)/shard_map/all_gather | solution.py:50
  63.3 211.5 %all-gather.17.cloned.1.call-start = ((), (), s32[]{:S(2)}) async-start(), calls=%async_computation.12 | async-start | bytes 4718592 | tf_op jit(solution)/shard_map/all_gather | solution.py:134
  63.9 46.9 %copy-start.38 = (bf16[2048,128]{1,0:T(8,128)(2,1)S(1)}, bf16[2048,128]{1,0:T(8,128)(2,1)}, u32[]{:S(2)}) copy-start(bf16[2048,128]{1,0:T(8,128)(2,1)} %param.34) | copy-start | bytes 1572868
  63.9 288.5 %all-gather.15.cloned.1.call-start = ((), (), s32[]{:S(2)}) async-start(), calls=%async_computation.10 | async-start | bytes 14417920 | tf_op jit(solution)/shard_map/all_gather | solution.py:57
  64.5 451.9 %all-reduce.10.cloned.1.call-start = ((), (), s32[]{:S(2)}) async-start(), calls=%async_computation.8 | async-start | bytes 12582912 | tf_op jit(solution)/shard_map/psum | solution.py:166
  64.5 127.2 %copy-start.54 = (f32[2048]{0:T(1024)}, f32[2048]{0:T(1024)S(1)}, u32[]{:S(2)}) copy-start(f32[2048]{0:T(1024)S(1)} %convert_element_type.128) | copy-start | bytes 24580
  110.9 80.9 %copy-start.46 = (f32[768]{0:T(1024)}, f32[768]{0:T(1024)S(1)}, u32[]{:S(2)}) copy-start(f32[768]{0:T(1024)S(1)} %add_rsqrt_fusion.1) | copy-start | bytes 9220
  111.9 93.4 %copy-start.41 = (bf16[768,128,1]{1,0,2:T(8,128)(2,1)}, bf16[768,128,1]{1,0,2:T(8,128)(2,1)S(1)}, u32[]{:S(2)}) copy-start(bf16[768,128,1]{1,0,2:T(8,128)(2,1)S(1)} %fusion.32) | copy-start | bytes 589828
  111.9 93.4 %copy-start.28 = (bf16[3,128,1024]{2,1,0:T(8,128)(2,1)S(1)}, bf16[3,128,1024]{2,1,0:T(8,128)(2,1)}, u32[]{:S(2)}) copy-start(bf16[3,128,1024]{2,1,0:T(8,128)(2,1)} %param.35) | copy-start | bytes 2359300
  207.3 4.7 collective-permute-start
  215.4 152.8 %copy-start.7 = (bf16[768,1024]{1,0:T(8,128)(2,1)}, bf16[768,1024]{1,0:T(8,128)(2,1)S(1)}, u32[]{:S(2)}) copy-start(bf16[768,1024]{1,0:T(8,128)(2,1)S(1)} %get-tuple-element.50) | copy-start | bytes 4718596
  235.2 39.5 %copy-start.44 = (bf16[128,2048]{1,0:T(8,128)(2,1)S(1)}, bf16[128,2048]{1,0:T(8,128)(2,1)}, u32[]{:S(2)}) copy-start(bf16[128,2048]{1,0:T(8,128)(2,1)} %param.41) | copy-start | bytes 1572868
  235.2 424.6 %all-gather.13.cloned.1.call-start = ((), (), s32[]{:S(2)}) async-start(), calls=%async_computation.9 | async-start | bytes 28835840 | tf_op jit(solution)/shard_map/all_gather | solution.py:56
  236.0 673.7 %all-reduce.16.cloned.1.call-start = ((), (), s32[]{:S(2)}) async-start(), calls=%async_computation.15 | async-start | bytes 14155776 | tf_op jit(solution)/shard_map/psum | solution.py:228
  352.3 15.8 %copy-start.32 = (bf16[1024,128]{1,0:T(8,128)(2,1)S(1)}, bf16[1024,128]{1,0:T(8,128)(2,1)}, u32[]{:S(2)}) copy-start(bf16[1024,128]{1,0:T(8,128)(2,1)} %param.36) | copy-start | bytes 786436
  368.2 148.1 %copy-start.14 = (bf16[128,2048]{1,0:T(8,128)(2,1)S(1)}, bf16[128,2048]{1,0:T(8,128)(2,1)}, u32[]{:S(2)}) copy-start(bf16[128,2048]{1,0:T(8,128)(2,1)} %param.37) | copy-start | bytes 1572868
  395.0 126.0 %copy-start.16 = (bf16[768,128]{1,0:T(8,128)(2,1)}, bf16[768,128]{1,0:T(8,128)(2,1)S(1)}, u32[]{:S(2)}) copy-start(bf16[768,128]{1,0:T(8,128)(2,1)S(1)} %all-reduce.17) | copy-start | bytes 589828
  739.0 290.9 %reduce-scatter.2.cloned.1.call-start = ((), (), s32[]{:S(2)}) async-start(), calls=%async_computation.11 | async-start | bytes 4718592 | tf_op jit(solution)/shard_map/reduce_scatter | solution.py:188
  753.5 156.2 %copy-start.26 = (f32[768,128]{1,0:T(8,128)S(1)}, f32[768,128]{1,0:T(8,128)}, u32[]{:S(2)}) copy-start(f32[768,128]{1,0:T(8,128)} %compare_convert_fusion) | copy-start | bytes 1179652
  753.5 156.2 %copy-start.31 = (bf16[2048,256]{1,0:T(8,128)(2,1)S(1)}, bf16[2048,256]{1,0:T(8,128)(2,1)}, u32[]{:S(2)}) copy-start(bf16[2048,256]{1,0:T(8,128)(2,1)} %param.38) | copy-start | bytes 3145732
  753.5 374.3 %all-reduce.12.cloned.1.call-start = ((), (), s32[]{:S(2)}) async-start(), calls=%async_computation.13 | async-start | bytes 12582912 | tf_op jit(solution)/shard_map/psum | solution.py:266
  929.3 5.5 collective-permute-start.1
  955.0 401.1 %all-reduce.14.cloned.1.call-start = ((), (), s32[]{:S(2)}) async-start(), calls=%async_computation.14 | async-start | bytes 23330816 | tf_op jit(solution)/shard_map/psum | solution.py:288
  978.8 45.0 %copy-start.47 = (f32[768]{0:T(1024)S(1)}, f32[768]{0:T(1024)}, u32[]{:S(2)}) copy-start(f32[768]{0:T(1024)} %copy-done.46) | copy-start | bytes 9220
  978.8 45.0 %copy-start.55 = (f32[2048]{0:T(1024)S(1)}, f32[2048]{0:T(1024)}, u32[]{:S(2)}) copy-start(f32[2048]{0:T(1024)} %copy-done.54) | copy-start | bytes 24580
  1033.2 94.6 %copy-start.39 = (bf16[2048,128]{1,0:T(8,128)(2,1)S(1)}, bf16[2048,128]{1,0:T(8,128)(2,1)}, u32[]{:S(2)}) copy-start(bf16[2048,128]{1,0:T(8,128)(2,1)} %param.34) | copy-start | bytes 1572868
  1180.9 178.3 %all-to-all-start.3 = ((bf16[4,192,1024]{2,1,0:T(8,128)(2,1)}), bf16[4,192,1024]{2,1,0:T(8,128)(2,1)}, u32[]{:S(2)}, u32[]{:S(2)}) async-start(bf16[4,192,1024]{2,1,0:T(8,128)(2,1)} %get-tuple-element.66), calls=%async_computation.4 | async-start | bytes 3145728 | tf_op jit(solution)/shard_map/all_to_all | solution.py:282
  (56 other events, 240.8 us)
Sparse Core Ops, SparseCore 0:
  61.9 46.0 all-gather.6
  109.6 82.0 all-gather.8
  193.3 34.4 all-gather.10
  229.8 44.9 all-gather.16
  276.2 76.1 all-gather.14
  354.6 161.6 all-reduce.9
  518.0 141.8 all-gather.12
  739.1 170.5 all-reduce.15
  911.9 43.3 reduce-scatter.1
  957.7 170.0 all-reduce.11
  1133.8 222.3 all-reduce.13
where the time goes:
time: 1390 us; the launch traced here: 1380 us
  waiting for transfers between devices  944 us (68%)
  matrix products  208 us (15%)
  blocking collectives  132 us (9%)
  local copies, waits for them, and re-layouts  36.4 us (3%)
  other arithmetic  31.6 us (2%)
  between operations  15.3 us (1%)
    psum x1, waiting for transfers between devices, body(): lax.psum((in_shrink_grad, input_expand_gradient, out_shrink_grad, output_...  171 us
    psum x1, waiting for transfers between devices, body(): lax.psum((ffn_in_part, feedforward_rank_part), 'tensor')  156 us
    all_gather x1, waiting for transfers between devices, fetch_ffn(): lax.all_gather(gateup_weight, 'dp', axis=1, tiled=True)  132 us
    psum x1, waiting for transfers between devices, body(): lax.psum((product_simple(gated_rows, out_full), product_simple(gated_rows...  121 us
    psum x1, waiting for transfers between devices, body(): lax.psum((normed_part, input_rank_part), 'tensor')  92.8 us
    all_gather x1, waiting for transfers between devices, fetch_mixer(): lax.all_gather(in_weight, 'dp', axis=1, tiled=True)  79.8 us
    all_gather x1, waiting for transfers between devices, fetch_ffn(): lax.all_gather(down_weight, 'dp', axis=1, tiled=True)  74 us
    dot_general x8, matrix products, product_backward(): lax.dot_general(left, right, (((1,), (1,)), ((), ())), preferred_element_...  49.3 us
  transfers between devices with their start and end apart: 15, of which 13 were waited for; matrix products, arithmetic and copies ran while one was open for 12% of the time, Pallas kernels for 0%

commit v1 on v0

--- a/solution.py
+++ b/solution.py
@@ -8,6 +8,19 @@
 adapter_scale = 0.5
 
 
+def ring_gather(x, axis, dim):
+    ways = lax.axis_size(axis)
+    up = [(d, (d + 1) % ways) for d in range(ways)]
+    down = [(d, (d - 1) % ways) for d in range(ways)]
+    earlier, later = ([x], [x])
+    for _ in range(ways // 2):
+        earlier.append(lax.ppermute(earlier[-1], axis, up))
+    for _ in range((ways - 1) // 2):
+        later.append(lax.ppermute(later[-1], axis, down))
+    line = jnp.concatenate([*earlier[::-1], *later[1:]], axis=dim)
+    return jnp.roll(line, (lax.axis_index(axis) - ways // 2) * x.shape[dim], axis=dim)
+
+
 def shifted(block, axis, distance):
     devices = range(lax.axis_size(axis))
     route = [(i - distance, i) for i in devices if i - distance in devices]
@@ -54,7 +67,7 @@
 def fetch_ffn(gateup_weight, down_weight):
     return (
         lax.all_gather(gateup_weight, "dp", axis=1, tiled=True),
-        lax.all_gather(down_weight, "dp", axis=1, tiled=True),
+        ring_gather(down_weight, "dp", 1),
     )
 
 

time: 1390 us -> 1320 us (0.950)
  waiting for transfers between devices: 944 us -> 840 us
  other arithmetic: 31.6 us -> 55.6 us
    ppermute x0 -> x3, waiting for transfers between devices: none -> 87.7 us  [the longest x2 87.7 us: ring_gather(): earlier.append(lax.ppermute(earlier[-1], axis, up))]
    psum x1, waiting for transfers between devices: 121 us -> 47.1 us  [body(): lax.psum((product_simple(gated_rows, out_full), product_simple(gated_rows...]
    all_gather x1 -> x0, waiting for transfers between devices: 74 us -> none  [fetch_ffn(): lax.all_gather(down_weight, 'dp', axis=1, tiled=True)]
    all_gather x1, waiting for transfers between devices: 36.9 us -> 0.01 us  [body(): lax.all_gather(packed_cot, 'tensor', axis=1, tiled=True)]
    concatenate x0 -> x1, other arithmetic: none -> 19.6 us  [ring_gather(): jnp.roll(line, (lax.axis_index(axis) - ways // 2) * x.shape[dim], axis=dim)]
  transfers between devices with their start and end apart: 15 -> 17, of which waited for: 13 -> 13; matrix products, arithmetic and copies ran while one was open for 12% -> 14% of each run, Pallas kernels for 0% -> 0%
where the time goes in v1:
time: 1320 us; the launch traced here: 1310 us
  waiting for transfers between devices  840 us (64%)
  matrix products  205 us (16%)
  blocking collectives  130 us (10%)
  other arithmetic  55.6 us (4%)
  local copies, waits for them, and re-layouts  36.4 us (3%)
  starting transfers between devices  27.1 us (2%)
  between operations  15.4 us (1%)
    psum x1, waiting for transfers between devices, body(): lax.psum((in_shrink_grad, input_expand_gradient, out_shrink_grad, output_...  171 us
    psum x1, waiting for transfers between devices, body(): lax.psum((ffn_in_part, feedforward_rank_part), 'tensor')  156 us
    all_gather x1, waiting for transfers between devices, fetch_ffn(): lax.all_gather(gateup_weight, 'dp', axis=1, tiled=True)  132 us
    psum x1, waiting for transfers between devices, body(): lax.psum((normed_part, input_rank_part), 'tensor')  88.4 us
    ppermute x2, waiting for transfers between devices, ring_gather(): earlier.append(lax.ppermute(earlier[-1], axis, up))  87.7 us
    all_gather x1, waiting for transfers between devices, fetch_mixer(): lax.all_gather(in_weight, 'dp', axis=1, tiled=True)  78.1 us
    psum x1, waiting for transfers between devices, body(): lax.psum((product_simple(gated_rows, out_full), product_simple(gated_rows...  47.1 us
    dot_general x8, matrix products, product_backward(): lax.dot_general(left, right, (((1,), (1,)), ((), ())), preferred_element_...  46.9 us
  transfers between devices with their start and end apart: 17, of which 13 were waited for; matrix products, arithmetic and copies ran while one was open for 14% of the time, Pallas kernels for 0%

profile of v1, /device:TPU:0, one launch (start us, length us, event | category | flops | bytes accessed | tf_op | source)
XLA Modules:
  0.0 1309.4 jit_solution(7512923251683657324)
XLA Ops:
  7.2 25.2 %all_to_all.20 = bf16[4,192,1024]{2,1,0:T(8,128)(2,1)} all-to-all(bf16[4,192,1024]{2,1,0:T(8,128)(2,1)} %bitcast.155), channel_id=1, replica_groups=mesh['dp'=4,'ctx'=4,'tensor'=2] {'dp'}, dimensions={0} | all-to-all | bytes 3145728 | tf_op jit(solution)/shard_map/all_to_all | solution.py:108
  39.3 16.8 %all-to-all-done.2 = bf16[4,192,1024]{2,1,0:T(8,128)(2,1)S(1)} async-done(((bf16[4,192,1024]{2,1,0:T(8,128)(2,1)}), bf16[4,192,1024]{2,1,0:T(8,128)(2,1)S(1)}, u32[]{:S(2)}, u32[]{:S(2)}) %all-to-all-start.2) | async-done | bytes 1572896 | tf_op jit(solution)/shard_map/all_to_all | solution.py:115
  64.5 43.5 %all-gather.6.cloned.1.call-done = bf16[768,2048]{1,0:T(8,128)(2,1)} async-done(((bf16[768,1024]{1,0:T(8,128)(2,1)}), bf16[768,2048]{1,0:T(8,128)(2,1)}) %all-gather.6.cloned.1.call-update) | async-done | bytes 3145744 | tf_op jit(solution)/shard_map/all_gather | solution.py:146
  113.6 78.1 %all-gather.8.cloned.1.call-done = bf16[3,2048,1024]{2,1,0:T(8,128)(2,1)} async-done(((bf16[3,512,1024]{2,1,0:T(8,128)(2,1)}), bf16[3,2048,1024]{2,1,0:T(8,128)(2,1)}) %all-gather.8.cloned.1.call-update) | async-done | bytes 12582928 | tf_op jit(solution)/shard_map/all_gather | solution.py:62
  191.7 13.6 %fusion.24 = f32[768,3,1024]{2,0,1:T(8,128)S(1)} fusion(bf16[3,2048,1024]{2,1,0:T(8,128)(2,1)} %all-gather.8.cloned.1.call-done, f32[2048]{0:T(1024)S(1)} %convert_element_type.128, f32[768]{0:T(1024)S(1)} %add_rsqrt_fusion.1, bf16[768,2048]{1,0:T(8,128)(2,1)} %all-gather.6.cloned.1.call-done), kind=kOutput, calls=%fused_computation.74 | convolution fusion | flops 9669967872 | bytes 25177088 | tf_op jit(solution)/shard_map/px,sxa->psa/dot_general | solution.py:162
  215.4 12.4 all-gather.10.cloned.1.call-done
  227.8 7.4 fusion.80
  237.7 62.8 %collective-permute-done.1 = bf16[2816,512]{1,0:T(8,128)(2,1)} collective-permute-done((bf16[2816,512]{1,0:T(8,128)(2,1)}, bf16[2816,512]{1,0:T(8,128)(2,1)}, u32[]{:S(2)}, u32[]{:S(2)}) %collective-permute-start.1) | collective-permute-done | bytes 2883616 | tf_op jit(solution)/shard_map/ppermute | solution.py:17
  300.5 12.1 collective-permute-start.2
  317.2 4.7 fusion.83
  321.9 24.9 %collective-permute-done.2 = bf16[2816,512]{1,0:T(8,128)(2,1)} collective-permute-done((bf16[2816,512]{1,0:T(8,128)(2,1)}, bf16[2816,512]{1,0:T(8,128)(2,1)}, u32[]{:S(2)}, u32[]{:S(2)}) %collective-permute-start.2) | collective-permute-done | bytes 2883616 | tf_op jit(solution)/shard_map/ppermute | solution.py:17
  346.8 19.6 %fusion.3 = bf16[2816,2048]{1,0:T(8,128)(2,1)} fusion(s32[]{:T(128)S(6)} %select_n.72, bf16[2816,512]{1,0:T(8,128)(2,1)} %collective-permute-done.2, bf16[2816,512]{1,0:T(8,128)(2,1)} %collective-permute-done.1, bf16[2816,512]{1,0:T(8,128)(2,1)S(1)} %copy-done.12, bf16[2816,512]{1,0:T(8,128)(2,1)} %collective-permute-done.3), kind=kLoop, calls=%fused_computation.16 | loop fusion | flops 92274688 | bytes 23068676 | tf_op jit(solution)/shard_map/jit(_roll_dynamic)/concatenate | solution.py:21
  367.7 23.9 %all-reduce.17 = bf16[768,128]{1,0:T(8,128)(2,1)S(1)} all-reduce(f32[768,128]{1,0:T(8,128)} %fusion.81), channel_id=1, replica_groups=mesh['dp'=4,'ctx'=4,'tensor'=2] {'tensor'}, use_global_device_ids=true, to_apply=%region_7.9 | all-reduce | flops 98304 | bytes 589824 | tf_op jit(solution)/shard_map/psum | solution.py:179
  391.6 47.1 %all-reduce.10.cloned.1.call-done = f32[768,2048]{1,0:T(8,128)} async-done(((f32[768,2048]{1,0:T(8,128)}), f32[768,2048]{1,0:T(8,128)}) %all-reduce.10.cloned.1.call-update) | async-done | bytes 6291472 | tf_op jit(solution)/shard_map/psum | solution.py:179
  438.7 4.7 multiply_reduce_fusion.2
  450.0 132.1 %all-gather.12.cloned.1.call-done = bf16[2,2048,2816]{2,1,0:T(8,128)(2,1)} async-done(((bf16[2,512,2816]{2,1,0:T(8,128)(2,1)}), bf16[2,2048,2816]{2,1,0:T(8,128)(2,1)}) %all-gather.12.cloned.1.call-update) | async-done | bytes 23068688 | tf_op jit(solution)/shard_map/all_gather | solution.py:69
  582.1 23.8 %fusion.22 = f32[768,2,2816]{2,0,1:T(8,128)S(1)} fusion(bf16[2,2048,2816]{2,1,0:T(8,128)(2,1)} %all-gather.12.cloned.1.call-done, bf16[768,2048]{1,0:T(8,128)(2,1)} %copy-done.10), kind=kOutput, calls=%fused_computation.72 | convolution fusion | flops 17716740096 | bytes 43515904 | tf_op jit(solution)/shard_map/cm,ame->cae/dot_general | solution.py:193
  605.9 8.4 bitcast_add_fusion
  614.3 22.8 %fusion.9 = (bf16[768,1,2816]{2,0,1:T(8,128)(2,1)}, bf16[768,1,2816]{2,0,1:T(8,128)(2,1)}, bf16[768,2816]{1,0:T(8,128)(2,1)}) fusion(f32[768,2,2816]{2,0,1:T(8,128)} %bitcast_add_fusion, f32[768,2816]{1,0:T(8,128)} %fusion.83, bf16[768,2048]{1,0:T(8,128)(2,1)} %all-gather.14.cloned.1.call-done, bf16[2816,2048]{1,0:T(8,128)(2,1)} %fusion.3), kind=kOutput, calls=%fused_computation.43 | convolution fusion | flops 8895135744 | bytes 53608448 | tf_op jit(solution)/shard_map/dot_general | solution.py:45
  637.1 5.1 fusion.31
  643.3 25.0 %convolution_bitcast_fusion.1 = f32[768,2048]{1,0:T(8,128)} fusion(bf16[2,2048,2816]{2,1,0:T(8,128)(2,1)} %all-gather.12.cloned.1.call-done, bf16[768,1,2816]{2,0,1:T(8,128)(2,1)} %get-tuple-element.54, bf16[768,1,2816]{2,0,1:T(8,128)(2,1)} %get-tuple-element.53), kind=kOutput, calls=%fused_computation.46 | convolution fusion | flops 17721065472 | bytes 38010880 | tf_op jit(solution)/shard_map/tjf,jdf->td/dot_general | solution.py:240
  668.4 14.4 %convolution_convert_fusion = bf16[768,2048]{1,0:T(8,128)(2,1)} fusion(bf16[768,2816]{1,0:T(8,128)(2,1)} %get-tuple-element.55, bf16[2816,2048]{1,0:T(8,128)(2,1)} %fusion.3), kind=kOutput, calls=%fused_computation.47 | convolution fusion | flops 8859942912 | bytes 19005440 | tf_op jit(solution)/shard_map/dot_general | solution.py:41
  682.9 156.2 %all-reduce.16.cloned.1.call-done = (f32[768,2048]{1,0:T(8,128)}, f32[768,256]{1,0:T(8,128)}) async-done(((f32[768,2048]{1,0:T(8,128)}, f32[768,256]{1,0:T(8,128)}), (f32[768,2048]{1,0:T(8,128)}, f32[768,256]{1,0:T(8,128)})) %all-reduce.16.cloned.1.call-update) | async-done | bytes 7077904 | tf_op jit(solution)/shard_map/psum | solution.py:241
  839.1 6.5 multiply_reduce_fusion.1
  870.0 14.8 %convolution_bitcast_fusion = f32[768,2048]{1,0:T(8,128)} fusion(bf16[3,2048,1024]{2,1,0:T(8,128)(2,1)} %all-gather.8.cloned.1.call-done, bf16[768,1,1024]{2,0,1:T(8,128)(2,1)S(1)} %fusion.30, bf16[768,1,1024]{2,0,1:T(8,128)(2,1)S(1)} %get-tuple-element.58, bf16[768,1,1024]{2,0,1:T(8,128)(2,1)S(1)} %get-tuple-element.49), kind=kOutput, calls=%fused_computation.45 | convolution fusion | flops 9668395008 | bytes 23592960 | tf_op jit(solution)/shard_map/tjc,jdc->td/dot_general | solution.py:278
  890.2 4.8 fusion.85
  895.0 6.8 convolution_multiply_fusion
  909.6 40.9 %all-reduce.18 = (bf16[768,128]{1,0:T(8,128)(2,1)S(1)}, bf16[768,128]{1,0:T(8,128)(2,1)S(1)}) all-reduce(f32[768,128]{1,0:T(8,128)S(1)} %copy-done.31, f32[768,128]{1,0:T(8,128)S(1)} %fusion.34), channel_id=1, replica_groups=mesh['dp'=4,'ctx'=4,'tensor'=2] {'tensor'}, use_global_device_ids=true, to_apply=%region_10.13 | all-reduce | flops 196608 | bytes 1179648 | tf_op jit(solution)/shard_map/psum | solution.py:207
  969.0 88.4 %all-reduce.12.cloned.1.call-done = f32[768,2048]{1,0:T(8,128)} async-done(((f32[768,2048]{1,0:T(8,128)}), f32[768,2048]{1,0:T(8,128)}) %all-reduce.12.cloned.1.call-update) | async-done | bytes 6291472 | tf_op jit(solution)/shard_map/psum | solution.py:279
  1057.4 4.9 multiply_reduce_fusion
  1070.7 39.8 %all_to_all.21 = bf16[4,192,1024]{2,1,0:T(8,128)(2,1)S(1)} all-to-all(bf16[4,192,1024]{2,1,0:T(8,128)(2,1)S(1)} %get-tuple-element.68), channel_id=1, replica_groups=mesh['dp'=4,'ctx'=4,'tensor'=2] {'dp'}, dimensions={0} | all-to-all | bytes 3145728 | tf_op jit(solution)/shard_map/all_to_all | solution.py:291
  1114.9 170.6 %all-reduce.14.cloned.1.call-done = (f32[2048,128]{1,0:T(8,128)}, f32[3,128,1024]{1,2,0:T(8,128)}, f32[1024,128]{1,0:T(8,128)}, f32[128,2048]{1,0:T(8,128)}, f32...) async-done(((f32[2048,128]{1,0:T(8,128)}, f32[3,128,1024]{1,2,0:T(8,128)}, f32[1024,128]{1,0:T(8,128)}, ...) | async-done | bytes 11665424 | tf_op jit(solution)/shard_map/psum | solution.py:301
  (273 shorter events, 131.9 us)
Async XLA Ops:
  7.2 598.7 %copy-start = (bf16[2,128,2816]{2,1,0:T(8,128)(2,1)S(1)}, bf16[2,128,2816]{2,1,0:T(8,128)(2,1)}, u32[]{:S(2)}) copy-start(bf16[2,128,2816]{2,1,0:T(8,128)(2,1)} %param.41) | copy-start | bytes 4325380
  32.4 23.6 %all-to-all-start.2 = ((bf16[4,192,1024]{2,1,0:T(8,128)(2,1)}), bf16[4,192,1024]{2,1,0:T(8,128)(2,1)S(1)}, u32[]{:S(2)}, u32[]{:S(2)}) async-start(bf16[4,192,1024]{2,1,0:T(8,128)(2,1)} %bitcast.156), calls=%async_computation.3 | async-start | bytes 3145728 | tf_op jit(solution)/shard_map/all_to_all | solution.py:115
  36.0 72.0 %all-gather.6.cloned.1.call-start = ((), (), s32[]{:S(2)}) async-start(), calls=%async_computation.5 | async-start | bytes 4718592 | tf_op jit(solution)/shard_map/all_gather | solution.py:146
  61.8 129.9 %all-gather.8.cloned.1.call-start = ((), (), s32[]{:S(2)}) async-start(), calls=%async_computation.6 | async-start | bytes 15728640 | tf_op jit(solution)/shard_map/all_gather | solution.py:62
  62.5 165.3 %all-gather.10.cloned.1.call-start = ((), (), s32[]{:S(2)}) async-start(), calls=%async_computation.7 | async-start | bytes 5242880 | tf_op jit(solution)/shard_map/all_gather | solution.py:63
  63.3 250.9 %all-gather.14.cloned.1.call-start = ((), (), s32[]{:S(2)}) async-start(), calls=%async_computation.11 | async-start | bytes 4718592 | tf_op jit(solution)/shard_map/all_gather | solution.py:147
  63.3 128.4 %copy-start.62 = (f32[2048]{0:T(1024)}, f32[2048]{0:T(1024)S(1)}, u32[]{:S(2)}) copy-start(f32[2048]{0:T(1024)S(1)} %convert_element_type.128) | copy-start | bytes 24580
  63.5 375.1 %copy-start.64 = (s32[128]{0:T(128)}, s32[128]{0:T(128)S(1)}, u32[]{:S(2)}) copy-start(s32[128]{0:T(128)S(1)} %and_select_fusion) | copy-start | bytes 1540
  63.8 374.9 %copy-start.48 = (s32[768]{0:T(1024)}, s32[768]{0:T(1024)S(1)}, u32[]{:S(2)}) copy-start(s32[768]{0:T(1024)S(1)} %select_reduce_fusion) | copy-start | bytes 9220
  64.4 374.3 %all-reduce.10.cloned.1.call-start = ((), (), s32[]{:S(2)}) async-start(), calls=%async_computation.8 | async-start | bytes 12582912 | tf_op jit(solution)/shard_map/psum | solution.py:179
  110.6 81.1 %copy-start.54 = (f32[768]{0:T(1024)}, f32[768]{0:T(1024)S(1)}, u32[]{:S(2)}) copy-start(f32[768]{0:T(1024)S(1)} %add_rsqrt_fusion.1) | copy-start | bytes 9220
  113.6 91.8 %copy-start.50 = (bf16[768,128,1]{1,0,2:T(8,128)(2,1)}, bf16[768,128,1]{1,0,2:T(8,128)(2,1)S(1)}, u32[]{:S(2)}) copy-start(bf16[768,128,1]{1,0,2:T(8,128)(2,1)S(1)} %fusion.39) | copy-start | bytes 589828
  113.6 91.8 %copy-start.33 = (bf16[3,128,1024]{2,1,0:T(8,128)(2,1)S(1)}, bf16[3,128,1024]{2,1,0:T(8,128)(2,1)}, u32[]{:S(2)}) copy-start(bf16[3,128,1024]{2,1,0:T(8,128)(2,1)} %param.37) | copy-start | bytes 2359300
  207.3 4.7 collective-permute-start
  215.4 150.9 %copy-start.6 = (bf16[768,1024]{1,0:T(8,128)(2,1)}, bf16[768,1024]{1,0:T(8,128)(2,1)S(1)}, u32[]{:S(2)}) copy-start(bf16[768,1024]{1,0:T(8,128)(2,1)S(1)} %get-tuple-element.51) | copy-start | bytes 4718596
  235.2 79.0 %copy-start.52 = (bf16[128,2048]{1,0:T(8,128)(2,1)S(1)}, bf16[128,2048]{1,0:T(8,128)(2,1)}, u32[]{:S(2)}) copy-start(bf16[128,2048]{1,0:T(8,128)(2,1)} %param.43) | copy-start | bytes 1572868
  235.3 346.9 %all-gather.12.cloned.1.call-start = ((), (), s32[]{:S(2)}) async-start(), calls=%async_computation.9 | async-start | bytes 28835840 | tf_op jit(solution)/shard_map/all_gather | solution.py:69
  235.8 603.3 %all-reduce.16.cloned.1.call-start = ((), (), s32[]{:S(2)}) async-start(), calls=%async_computation.14 | async-start | bytes 14155776 | tf_op jit(solution)/shard_map/psum | solution.py:241
  235.9 64.6 %collective-permute-start.1 = (bf16[2816,512]{1,0:T(8,128)(2,1)}, bf16[2816,512]{1,0:T(8,128)(2,1)}, u32[]{:S(2)}, u32[]{:S(2)}) collective-permute-start(bf16[2816,512]{1,0:T(8,128)(2,1)} %param.35), channel_id=1, source_target_pairs={{0,8},{8,16},{16,24},{24,0},{1,9},{9,17},{17,25},{25,1},{2,10},{10... | collective-permute-start | bytes 8650760 | tf_op jit(solution)/shard_map/ppermute | solution.py:17
  236.2 85.7 %collective-permute-start.3 = (bf16[2816,512]{1,0:T(8,128)(2,1)}, bf16[2816,512]{1,0:T(8,128)(2,1)}, u32[]{:S(2)}, u32[]{:S(2)}) collective-permute-start(bf16[2816,512]{1,0:T(8,128)(2,1)} %param.35), channel_id=1, source_target_pairs={{0,24},{8,0},{16,8},{24,16},{1,25},{9,1},{17,9},{25,17},{2,26},{10... | collective-permute-start | bytes 8650760 | tf_op jit(solution)/shard_map/ppermute | solution.py:19
  300.5 46.3 %collective-permute-start.2 = (bf16[2816,512]{1,0:T(8,128)(2,1)}, bf16[2816,512]{1,0:T(8,128)(2,1)}, u32[]{:S(2)}, u32[]{:S(2)}) collective-permute-start(bf16[2816,512]{1,0:T(8,128)(2,1)} %collective-permute-done.1), channel_id=1, source_target_pairs={{0,8},{8,16},{16,24},{24,0},{1,9},{9,17},{17,25},{25,1},{2,10},{10... | collective-permute-start | bytes 8650760 | tf_op jit(solution)/shard_map/ppermute | solution.py:17
  366.3 72.4 %copy-start.16 = (bf16[128,2048]{1,0:T(8,128)(2,1)S(1)}, bf16[128,2048]{1,0:T(8,128)(2,1)}, u32[]{:S(2)}) copy-start(bf16[128,2048]{1,0:T(8,128)(2,1)} %param.39) | copy-start | bytes 1572868
  391.6 51.8 %copy-start.19 = (bf16[768,128]{1,0:T(8,128)(2,1)}, bf16[768,128]{1,0:T(8,128)(2,1)S(1)}, u32[]{:S(2)}) copy-start(bf16[768,128]{1,0:T(8,128)(2,1)S(1)} %all-reduce.17) | copy-start | bytes 589828
  450.0 155.9 %copy-start.21 = (bf16[768,256]{0,1:T(8,128)(2,1)}, bf16[768,256]{0,1:T(8,128)(2,1)S(1)}, u32[]{:S(2)}) copy-start(bf16[768,256]{0,1:T(8,128)(2,1)S(1)} %copy.45) | copy-start | bytes 1179652
  668.4 294.4 %reduce-scatter.2.cloned.1.call-start = ((), (), s32[]{:S(2)}) async-start(), calls=%async_computation.10 | async-start | bytes 4718592 | tf_op jit(solution)/shard_map/reduce_scatter | solution.py:201
  682.8 156.2 %copy-start.30 = (f32[768,128]{1,0:T(8,128)S(1)}, f32[768,128]{1,0:T(8,128)}, u32[]{:S(2)}) copy-start(f32[768,128]{1,0:T(8,128)} %compare_convert_fusion) | copy-start | bytes 1179652
  682.8 156.2 %copy-start.38 = (bf16[2048,256]{1,0:T(8,128)(2,1)S(1)}, bf16[2048,256]{1,0:T(8,128)(2,1)}, u32[]{:S(2)}) copy-start(bf16[2048,256]{1,0:T(8,128)(2,1)} %param.40) | copy-start | bytes 3145732
  682.9 374.5 %all-reduce.12.cloned.1.call-start = ((), (), s32[]{:S(2)}) async-start(), calls=%async_computation.12 | async-start | bytes 12582912 | tf_op jit(solution)/shard_map/psum | solution.py:279
  859.0 5.5 collective-permute-start.4
  884.8 400.6 %all-reduce.14.cloned.1.call-start = ((), (), s32[]{:S(2)}) async-start(), calls=%async_computation.13 | async-start | bytes 23330816 | tf_op jit(solution)/shard_map/psum | solution.py:301
  967.2 90.2 %copy-start.46 = (bf16[2048,128]{1,0:T(8,128)(2,1)S(1)}, bf16[2048,128]{1,0:T(8,128)(2,1)}, u32[]{:S(2)}) copy-start(bf16[2048,128]{1,0:T(8,128)(2,1)} %param.36) | copy-start | bytes 1572868
  1110.5 178.0 %all-to-all-start.3 = ((bf16[4,192,1024]{2,1,0:T(8,128)(2,1)}), bf16[4,192,1024]{2,1,0:T(8,128)(2,1)}, u32[]{:S(2)}, u32[]{:S(2)}) async-start(bf16[4,192,1024]{2,1,0:T(8,128)(2,1)} %get-tuple-element.67), calls=%async_computation.4 | async-start | bytes 3145728 | tf_op jit(solution)/shard_map/all_to_all | solution.py:295
  (67 other events, 487.8 us)
Sparse Core Ops, SparseCore 0:
  61.9 46.0 all-gather.5
  109.6 82.0 all-gather.7
  193.3 34.4 all-gather.9
  229.8 44.9 all-gather.13
  277.0 161.6 all-reduce.9
  440.2 141.8 all-gather.11
  668.5 170.5 all-reduce.15
  841.3 43.3 reduce-scatter.1
  887.3 170.0 all-reduce.11
  1063.2 222.1 all-reduce.13
